TPU v7x, 128 devices: a whole 4x4x4 slice. The times are simulated.
128 devices in a mesh: row: 16 (over z, y_lo, core), col: 8 (over y_hi, x).
Axes of the slice: x: 4, y: 4 (y_hi: 2, y_lo: 2; y = y_hi * 2 + y_lo), z: 4, core: 2. Of those that a mesh axis runs over, the one named last changes fastest.
Arguments:
- panels: bfloat16 [1024, 32, 256], P(('row', 'col')), may hold values from -21 to 21
- tiles: bfloat16 [6144, 256, 512], P(('row', 'col')), may hold values from -0.109375 to 0.109375
- tile_dst: int32 [6144], P(('row', 'col')), may hold values from 0 to 7
- tile_src: int32 [6144], P(('row', 'col')), may hold values from 0 to 127
- geometry: float32 [1024, 6, 256], P(('row', 'col')), may hold values from -5 to 5
- areas: float32 [1024, 256], P(('row', 'col')), may hold values from 0.25 to 2
- block_owner: int32 [1024, 1], P(('row', 'col')), may hold values from 0 to 7; in each aligned block of 8 rows (0 to 7, 8 to 15, ...) at most 2 rows name the same one
- block_slot: int32 [1024], P(('row', 'col')), may hold values from 0 to 3
Outputs:
- field: float32 [1024, 32, 256], P(('row', 'col'))
- shape_gradient: float32 [1024, 256], P(('row', 'col'))
Inputs may be any that keep to these rules, and one draw needn't show every extreme that they name: Among the blocks of one device at most 2 have the same block_owner, and some device reaches 2.
All inputs are finite; a program needn't handle non-finite values.
Results may differ from a plain program's by a relative error of at most 0.0003.
Values may be sent and summed in bfloat16 or wider, within the bound.
A program may use at most 64 MiB of HBM per device.

v0:
```python
import jax
import jax.numpy as jnp
from jax import lax
from jax.sharding import PartitionSpec as P

CAP = 2
PD = 4
EPSILON = 1e-05


def make_basis(geometry, areas):
    normal = geometry[:, 0:3]
    place = geometry[:, 3:6]
    twist = jnp.stack(
        [
            place[:, 1] * normal[:, 2] - place[:, 2] * normal[:, 1],
            place[:, 2] * normal[:, 0] - place[:, 0] * normal[:, 2],
            place[:, 0] * normal[:, 1] - place[:, 1] * normal[:, 0],
        ],
        axis=1,
    )
    weight = areas[:, None, :]
    return jnp.concatenate([weight * normal, weight * twist, weight, weight], axis=1)


def split_complex(images, freq_count, node_count):
    real_part = images[:, :freq_count, :node_count] - images[:, freq_count:, node_count:]
    imag_part = images[:, :freq_count, node_count:] + images[:, freq_count:, :node_count]
    return jnp.concatenate([real_part, imag_part], axis=1)


def normalize(totals):
    return totals * lax.rsqrt(jnp.mean(totals * totals, axis=1, keepdims=True) + EPSILON)


def shards(panels, tiles, tile_dst, tile_src, geometry, areas, block_owner, block_slot):
    precise = lax.Precision.HIGHEST
    block_count, rows_twice, node_count = panels.shape
    freq_count = rows_twice // 2
    tile_count = tiles.shape[0]
    flat_panels = panels.reshape(block_count, rows_twice * node_count)
    gathered = lax.all_gather(flat_panels, "row", axis=0, tiled=True)
    count = gathered.shape[0]
    picking = (tile_src[:, None] == jnp.arange(count, dtype=jnp.int32)[None, :]).astype(
        jnp.bfloat16
    )
    picked = jnp.dot(picking, gathered, preferred_element_type=jnp.float32)
    chosen = picked.astype(jnp.bfloat16).reshape(tile_count, rows_twice, node_count)
    images = jnp.einsum("tjn,tnm->tjm", chosen, tiles, preferred_element_type=jnp.float32)
    tile_terms = split_complex(images, freq_count, node_count)
    target = (tile_dst[None, :] == jnp.arange(block_count, dtype=jnp.int32)[:, None]).astype(
        jnp.float32
    )
    near = jnp.einsum("dt,tjn->djn", target, tile_terms, precision=precise)
    incident = panels.astype(jnp.float32)
    field = 0.5 * incident + near
    power = field[:, :freq_count] ** 2 + field[:, freq_count:] ** 2
    cross_power = (
        incident[:, :freq_count] * field[:, :freq_count]
        + incident[:, freq_count:] * field[:, freq_count:]
    )
    basis = make_basis(geometry, areas)
    first_moments = jnp.einsum("bkn,bfn->bkf", basis[:, :7], power, precision=precise)
    last_moment = jnp.einsum("bn,bfn->bf", basis[:, 7], cross_power, precision=precise)
    moments = jnp.concatenate([first_moments, last_moment[:, None, :]], axis=1).reshape(
        block_count, -1
    )
    moment_width = moments.shape[1]
    group_count = lax.axis_size("col")
    owner = block_owner[:, 0]
    block_index = jnp.arange(block_count, dtype=jnp.int32)
    same_owner = owner[:, None] == owner[None, :]
    earlier = block_index[None, :] < block_index[:, None]
    rank = jnp.sum(jnp.where(same_owner & earlier, 1, 0), axis=1)
    slot_target = owner * CAP + rank
    slot_index = jnp.arange(group_count * CAP, dtype=jnp.int32)
    placing = slot_index[:, None] == slot_target[None, :]
    place_float = placing.astype(jnp.float32)
    send_values = jnp.dot(place_float, moments, precision=precise).reshape(
        group_count, CAP, moment_width
    )
    send_labels = (
        jnp.sum(jnp.where(placing, block_slot[None, :] + 1, 0), axis=1).astype(jnp.float32) - 1.0
    ).reshape(group_count, CAP)
    received, labels = (
        lax.all_to_all(send_values, "col", split_axis=0, concat_axis=0, tiled=True),
        lax.all_to_all(send_labels, "col", split_axis=0, concat_axis=0, tiled=True),
    )
    member = (
        labels.reshape(-1)[None, :] == jnp.arange(PD, dtype=jnp.int32).astype(jnp.float32)[:, None]
    ).astype(jnp.float32)
    totals = jnp.dot(member, received.reshape(-1, moment_width), precision=precise)
    adjoint = normalize(totals)
    answer = jnp.dot(member.T, adjoint, precision=precise).reshape(group_count, CAP, moment_width)
    returned = lax.all_to_all(answer, "col", split_axis=0, concat_axis=0, tiled=True)
    block_adjoint = jnp.dot(place_float.T, returned.reshape(-1, moment_width), precision=precise)
    shaped = block_adjoint.reshape(block_count, 8, freq_count)
    first_terms = jnp.einsum("bkf,bfn->bkn", shaped[:, :7], power, precision=precise)
    last_term = jnp.einsum("bf,bfn->bn", shaped[:, 7], cross_power, precision=precise)
    shape_gradient = (
        jnp.sum(basis[:, :7] * first_terms, axis=1) + basis[:, 7] * last_term
    ) / freq_count
    return (field, shape_gradient)


def solution(mesh):
    in_specs = (
        P(("row", "col"), None, None),
        P(("row", "col"), None, None),
        P(("row", "col")),
        P(("row", "col")),
        P(("row", "col"), None, None),
        P(("row", "col"), None),
        P(("row", "col"), None),
        P(("row", "col")),
    )
    out_specs = (P(("row", "col"), None, None), P(("row", "col"), None))
    return jax.shard_map(shards, mesh=mesh, in_specs=in_specs, out_specs=out_specs, check_vma=False)
```

profile of v0, /device:TPU:0, one launch (start us, length us, event | category | flops | bytes accessed | tf_op | source)
XLA Modules:
  0.0 94.8 jit_solution(7106194001397986972)
XLA Ops:
  7.2 1.6 %copy.87 = bf16[1,8,32,256]{3,1,2,0:T(8,128)(2,1)} copy(bf16[1,8,32,256]{3,2,1,0:T(8,128)(2,1)} %bitcast.44) | data formatting | bytes 262144
  8.9 0.9 select_reduce_fusion.1
  9.8 0.7 multiply_add_fusion.2
  10.6 0.7 sub.25
  11.2 7.0 %all-to-all-start = ((f32[8,1,2]{2,1,0:T(1,128)}), f32[8,1,2]{2,1,0:T(1,128)S(1)}, u32[]{:S(2)}, u32[]{:S(2)}) async-start(f32[8,1,2]{2,1,0:T(1,128)} %bitcast.3), calls=%async_computation | async-start | bytes 8192 | tf_op jit(solution)/shard_map/all_to_all | solution.py:87
  18.3 0.7 broadcast_in_dim.24
  19.0 0.7 slice.73
  19.7 0.8 fusion.42
  20.5 0.7 copy_multiply_fusion
  21.3 1.0 %copy_convert_fusion = f32[8,32,256]{2,0,1:T(8,128)S(1)} fusion(bf16[8,32,256]{2,1,0:T(8,128)(2,1)} %param.8), kind=kLoop, calls=%fused_computation.12 | loop fusion | flops 65536 | bytes 393216 | tf_op jit(solution)/shard_map/convert_element_type | solution.py:55
  22.3 24.3 %all-gather.2.cloned.1.call-done = bf16[128,8192]{1,0:T(8,128)(2,1)} async-done(((bf16[8,8192]{1,0:T(8,128)(2,1)}), bf16[128,8192]{1,0:T(8,128)(2,1)}) %all-gather.2.cloned.1.call-update) | async-done | bytes 2097168 | tf_op jit(solution)/shard_map/all_gather | solution.py:42
  46.6 2.1 %convolution_convert_fusion = bf16[48,8192]{1,0:T(8,128)(2,1)S(1)} fusion(bf16[128,8192]{1,0:T(8,128)(2,1)} %all-gather.2.cloned.1.call-done, s32[48]{0:T(128)} %param.11), kind=kOutput, calls=%fused_computation | convolution fusion | flops 101062656 | bytes 2883776 | tf_op jit(solution)/shard_map/dot_general | solution.py:47
  48.9 6.8 %fusion.43 = f32[48,32,512]{2,1,0:T(8,128)S(1)} fusion(bf16[48,32,256]{2,1,0:T(8,128)(2,1)S(1)} %bitcast.42, bf16[48,256,512]{2,1,0:T(8,128)(2,1)} %param.9), kind=kOutput, calls=%fused_computation.69 | convolution fusion | flops 402653184 | bytes 16515072 | tf_op jit(solution)/shard_map/tjn,tnm->tjm/dot_general | solution.py:49
  55.7 0.3 slice_subtract_fusion
  56.2 0.7 copy-done
  56.9 1.5 %fusion.2 = f32[8,32,256]{2,0,1:T(8,128)S(1)} fusion(f32[48,32,256]{2,1,0:T(8,128)S(1)} %pad_maximum_fusion, bf16[8,32,256]{2,1,0:T(8,128)(2,1)S(1)} %copy-done, s32[48]{0:T(128)S(1)} %copy-done.2), kind=kOutput, calls=%fused_computation.4 | convolution fusion | flops 37945728 | bytes 1966272 | tf_op jit(solution)/shard_map/dt,tjn->djn/dot_general | solution.py:54
  58.5 0.3 fusion.9
  58.8 0.3 fusion.12
  59.3 0.6 copy.70
  60.0 6.6 %all-to-all-start.1 = ((f32[8,2,128]{2,1,0:T(2,128)}), f32[8,2,128]{2,1,0:T(2,128)S(1)}, u32[]{:S(2)}, u32[]{:S(2)}) async-start(f32[8,2,128]{2,1,0:T(2,128)} %copy.70), calls=%async_computation.1 | async-start | bytes 16384 | tf_op jit(solution)/shard_map/all_to_all | solution.py:86
  66.5 0.5 broadcast.78
  67.0 0.7 reduce.3
  67.8 6.4 %all-to-all-done.1 = f32[8,2,128]{2,1,0:T(2,128)S(1)} async-done(((f32[8,2,128]{2,1,0:T(2,128)}), f32[8,2,128]{2,1,0:T(2,128)S(1)}, u32[]{:S(2)}, u32[]{:S(2)}) %all-to-all-start.1) | async-done | bytes 8224 | tf_op jit(solution)/shard_map/all_to_all | solution.py:86
  74.2 0.3 multiply_reduce_fusion
  74.5 0.9 fusion.29
  75.4 3.3 %all-to-all-start.2 = ((f32[8,2,128]{2,1,0:T(2,128)}), f32[8,2,128]{2,1,0:T(2,128)S(1)}, u32[]{:S(2)}, u32[]{:S(2)}) async-start(f32[8,2,128]{2,1,0:T(2,128)} %bitcast.10), calls=%async_computation.2 | async-start | bytes 16384 | tf_op jit(solution)/shard_map/all_to_all | solution.py:95
  78.7 0.8 copy.74
  79.5 6.8 %all-to-all-done.2 = f32[8,2,128]{2,1,0:T(2,128)S(1)} async-done(((f32[8,2,128]{2,1,0:T(2,128)}), f32[8,2,128]{2,1,0:T(2,128)S(1)}, u32[]{:S(2)}, u32[]{:S(2)}) %all-to-all-start.2) | async-done | bytes 8224 | tf_op jit(solution)/shard_map/all_to_all | solution.py:95
  86.5 0.4 fusion.26
  86.8 0.3 fusion.5
  87.1 0.2 fusion.7
  87.4 0.6 fusion.17
  (24 shorter events, 1.0 us)
Async XLA Ops:
  7.2 39.5 %all-gather.2.cloned.1.call-start = ((), (), s32[]{:S(2)}) async-start(), calls=%async_computation.3 | async-start | bytes 2228224 | tf_op jit(solution)/shard_map/all_gather | solution.py:42
  11.2 48.7 %all-to-all-start = ((f32[8,1,2]{2,1,0:T(1,128)}), f32[8,1,2]{2,1,0:T(1,128)S(1)}, u32[]{:S(2)}, u32[]{:S(2)}) async-start(f32[8,1,2]{2,1,0:T(1,128)} %bitcast.3), calls=%async_computation | async-start | bytes 8192 | tf_op jit(solution)/shard_map/all_to_all | solution.py:87
  56.0 0.9 copy-start
  56.0 0.9 copy-start.2
  56.9 1.6 %copy-start.1 = (f32[8,256]{1,0:T(8,128)S(1)}, f32[8,256]{1,0:T(8,128)}, u32[]{:S(2)}) copy-start(f32[8,256]{1,0:T(8,128)} %param.13) | copy-start | bytes 24580
  60.0 14.3 %all-to-all-start.1 = ((f32[8,2,128]{2,1,0:T(2,128)}), f32[8,2,128]{2,1,0:T(2,128)S(1)}, u32[]{:S(2)}, u32[]{:S(2)}) async-start(f32[8,2,128]{2,1,0:T(2,128)} %copy.70), calls=%async_computation.1 | async-start | bytes 16384 | tf_op jit(solution)/shard_map/all_to_all | solution.py:86
  75.4 11.0 %all-to-all-start.2 = ((f32[8,2,128]{2,1,0:T(2,128)}), f32[8,2,128]{2,1,0:T(2,128)S(1)}, u32[]{:S(2)}, u32[]{:S(2)}) async-start(f32[8,2,128]{2,1,0:T(2,128)} %bitcast.10), calls=%async_computation.2 | async-start | bytes 16384 | tf_op jit(solution)/shard_map/all_to_all | solution.py:95
Sparse Core Ops, SparseCore 0:
  10.2 36.3 all-gather.1
where the time goes:
time: 95.4 us; the launch traced here: 94.8 us
  waiting for transfers between devices  37.6 us (39%)
  starting transfers between devices  17 us (18%)
  between operations  14.2 us (15%)
  matrix products  13.1 us (14%)
  local copies, waits for them, and re-layouts  7.64 us (8%)
  other arithmetic  5.25 us (6%)
    all_gather x1, waiting for transfers between devices, shards(): gathered = lax.all_gather(flat_panels, 'row', axis=0, tiled=True)  24.3 us
    all_to_all x1, starting transfers between devices, shards(): lax.all_to_all(send_labels, 'col', split_axis=0, concat_axis=0, tiled=True)  7.04 us
    all_to_all x1, waiting for transfers between devices, shards(): lax.all_to_all(answer, 'col', split_axis=0, concat_axis=0, tiled=True)  6.84 us
    dot_general x1, matrix products, shards(): jnp.einsum('tjn,tnm->tjm', chosen, tiles, preferred_element_type=jnp.floa...  6.83 us
    all_to_all x1, starting transfers between devices, shards(): lax.all_to_all(send_values, 'col', split_axis=0, concat_axis=0, tiled=True)  6.56 us
    all_to_all x1, waiting for transfers between devices, shards(): lax.all_to_all(send_values, 'col', split_axis=0, concat_axis=0, tiled=True)  6.43 us
    unnamed x9, local copies, waits for them, and re-layouts  3.35 us
    all_to_all x1, starting transfers between devices, shards(): lax.all_to_all(answer, 'col', split_axis=0, concat_axis=0, tiled=True)  3.33 us
  transfers between devices with their start and end apart: 4, of which 3 were waited for; matrix products, arithmetic and copies ran while one was open for 22% of the time, Pallas kernels for 0%

commit v1 on v0

--- a/solution.py
+++ b/solution.py
@@ -39,7 +39,10 @@
     freq_count = rows_twice // 2
     tile_count = tiles.shape[0]
     flat_panels = panels.reshape(block_count, rows_twice * node_count)
-    gathered = lax.all_gather(flat_panels, "row", axis=0, tiled=True)
+    last = lax.all_to_all(
+        jnp.stack([flat_panels for _ in range(lax.axis_size("row"))]), "row", 0, 0
+    )
+    gathered = jnp.concatenate(last, axis=0)
     count = gathered.shape[0]
     picking = (tile_src[:, None] == jnp.arange(count, dtype=jnp.int32)[None, :]).astype(
         jnp.bfloat16

time: 95.4 us -> 84.8 us (0.89)
  between operations: 14.2 us -> 0.86 us
  starting transfers between devices: 17 us -> 23.9 us
  other arithmetic: 5.25 us -> 2.21 us
  waiting for transfers between devices: 37.6 us -> 39.9 us
  matrix products: 13.1 us -> 11.5 us
  local copies, waits for them, and re-layouts: 7.64 us -> 6.1 us
    all_to_all x0 -> x1, waiting for transfers between devices: none -> 26.6 us  [shards(): lax.all_to_all(jnp.stack([flat_panels for _ in range(lax.axis_size('row')...]
    all_gather x1 -> x0, waiting for transfers between devices: 24.3 us -> none  [shards(): gathered = lax.all_gather(flat_panels, 'row', axis=0, tiled=True)]
    all_to_all x0 -> x1, starting transfers between devices: none -> 6.69 us  [shards(): lax.all_to_all(jnp.stack([flat_panels for _ in range(lax.axis_size('row')...]
    dot_general x1, matrix products: 2.07 us -> 0.46 us  [shards(): picked = jnp.dot(picking, gathered, preferred_element_type=jnp.float32)]
    another operation x0 -> x1, local copies, waits for them, and re-layouts: none -> 1.54 us  [shards(): jnp.stack([flat_panels for _ in range(lax.axis_size('row'))])]
    unnamed x9 -> x17, local copies, waits for them, and re-layouts: 3.35 us -> 2.48 us
  transfers between devices with their start and end apart: 4 -> 4, of which waited for: 3 -> 3; matrix products, arithmetic and copies ran while one was open for 22% -> 17% of each run, Pallas kernels for 0% -> 0%
where the time goes in v1:
time: 84.8 us; the launch traced here: 84.4 us
  waiting for transfers between devices  39.9 us (47%)
  starting transfers between devices  23.9 us (28%)
  matrix products  11.5 us (14%)
  local copies, waits for them, and re-layouts  6.1 us (7%)
  other arithmetic  2.21 us (3%)
  between operations  0.86 us (1%)
    all_to_all x1, waiting for transfers between devices, shards(): lax.all_to_all(jnp.stack([flat_panels for _ in range(lax.axis_size('row')...  26.6 us
    all_to_all x1, starting transfers between devices, shards(): lax.all_to_all(send_values, 'col', split_axis=0, concat_axis=0, tiled=True)  7.2 us
    all_to_all x1, waiting for transfers between devices, shards(): lax.all_to_all(answer, 'col', split_axis=0, concat_axis=0, tiled=True)  6.84 us
    dot_general x1, matrix products, shards(): jnp.einsum('tjn,tnm->tjm', chosen, tiles, preferred_element_type=jnp.floa...  6.83 us
    all_to_all x1, starting transfers between devices, shards(): lax.all_to_all(jnp.stack([flat_panels for _ in range(lax.axis_size('row')...  6.69 us
    all_to_all x1, starting transfers between devices, shards(): lax.all_to_all(send_labels, 'col', split_axis=0, concat_axis=0, tiled=True)  6.64 us
    all_to_all x1, waiting for transfers between devices, shards(): lax.all_to_all(send_values, 'col', split_axis=0, concat_axis=0, tiled=True)  6.43 us
    all_to_all x1, starting transfers between devices, shards(): lax.all_to_all(answer, 'col', split_axis=0, concat_axis=0, tiled=True)  3.33 us
  transfers between devices with their start and end apart: 4, of which 3 were waited for; matrix products, arithmetic and copies ran while one was open for 17% of the time, Pallas kernels for 0%

profile of v1, /device:TPU:0, one launch (start us, length us, event | category | flops | bytes accessed | tf_op | source)
XLA Modules:
  0.0 84.4 jit_solution(12633867401170301511)
XLA Ops:
  0.6 1.0 %copy.87 = bf16[1,8,32,256]{3,1,2,0:T(8,128)(2,1)S(1)} copy(bf16[1,8,32,256]{3,2,1,0:T(8,128)(2,1)} %bitcast.46) | data formatting | bytes 262144
  1.6 1.5 %stack.4 = bf16[16,8,8192]{2,1,0:T(8,128)(2,1)} broadcast(bf16[8,8192]{1,0:T(8,128)(2,1)S(1)} %bitcast.47), dimensions={1,2} | broadcast | bytes 2228224 | tf_op jit(solution)/shard_map/stack | solution.py:43
  3.2 6.7 %all-to-all-start = ((bf16[16,8,8192]{2,1,0:T(8,128)(2,1)}), bf16[16,8,8192]{2,1,0:T(8,128)(2,1)S(1)}, u32[]{:S(2)}, u32[]{:S(2)}) async-start(bf16[16,8,8192]{2,1,0:T(8,128)(2,1)} %stack.4), calls=%async_computation | async-start | bytes 4194304 | tf_op jit(solution)/shard_map/all_to_all | solution.py:42
  9.9 0.2 select_reduce_fusion.1
  10.2 0.7 sub.25
  11.1 26.6 %all-to-all-done = bf16[16,8,8192]{2,1,0:T(8,128)(2,1)S(1)} async-done(((bf16[16,8,8192]{2,1,0:T(8,128)(2,1)}), bf16[16,8,8192]{2,1,0:T(8,128)(2,1)S(1)}, u32[]{:S(2)}, u32[]{:S(2)}) %all-to-all-start) | async-done | bytes 2097184 | tf_op jit(solution)/shard_map/all_to_all | solution.py:42
  37.7 6.6 %all-to-all-start.1 = ((f32[8,1,2]{2,1,0:T(1,128)}), f32[8,1,2]{2,1,0:T(1,128)S(1)}, u32[]{:S(2)}, u32[]{:S(2)}) async-start(f32[8,1,2]{2,1,0:T(1,128)} %bitcast.4), calls=%async_computation.1 | async-start | bytes 8192 | tf_op jit(solution)/shard_map/all_to_all | solution.py:90
  44.4 0.5 convolution_convert_fusion
  44.8 0.2 copy.88
  45.0 6.8 %fusion.44 = f32[48,32,512]{2,1,0:T(8,128)S(1)} fusion(bf16[48,32,256]{2,1,0:T(8,128)(2,1)S(1)} %bitcast.44, bf16[48,256,512]{2,1,0:T(8,128)(2,1)} %param.9), kind=kOutput, calls=%fused_computation.70 | convolution fusion | flops 402653184 | bytes 16515072 | tf_op jit(solution)/shard_map/tjn,tnm->tjm/dot_general | solution.py:52
  51.8 0.3 slice_subtract_fusion
  52.2 0.1 pad_maximum_fusion
  52.3 0.5 copy-done.4
  52.8 1.5 %fusion.3 = f32[8,32,256]{2,0,1:T(8,128)S(1)} fusion(f32[48,32,256]{2,1,0:T(8,128)S(1)} %pad_maximum_fusion, bf16[8,32,256]{2,1,0:T(8,128)(2,1)S(1)} %copy-done, s32[48]{0:T(128)S(1)} %copy-done.4), kind=kOutput, calls=%fused_computation.5 | convolution fusion | flops 37945728 | bytes 1966272 | tf_op jit(solution)/shard_map/dt,tjn->djn/dot_general | solution.py:57
  54.3 0.3 fusion.10
  54.6 0.3 fusion.13
  55.0 0.2 fusion.20
  55.2 0.6 copy.70
  55.8 7.2 %all-to-all-start.2 = ((f32[8,2,128]{2,1,0:T(2,128)}), f32[8,2,128]{2,1,0:T(2,128)S(1)}, u32[]{:S(2)}, u32[]{:S(2)}) async-start(f32[8,2,128]{2,1,0:T(2,128)} %copy.70), calls=%async_computation.2 | async-start | bytes 16384 | tf_op jit(solution)/shard_map/all_to_all | solution.py:89
  63.0 0.5 broadcast.79
  63.5 0.7 reduce.3
  64.3 6.4 %all-to-all-done.2 = f32[8,2,128]{2,1,0:T(2,128)S(1)} async-done(((f32[8,2,128]{2,1,0:T(2,128)}), f32[8,2,128]{2,1,0:T(2,128)S(1)}, u32[]{:S(2)}, u32[]{:S(2)}) %all-to-all-start.2) | async-done | bytes 8224 | tf_op jit(solution)/shard_map/all_to_all | solution.py:89
  70.7 0.3 multiply_reduce_fusion
  71.0 0.9 %fusion.30 = f32[16,128]{1,0:T(8,128)} fusion(f32[4,128]{1,0:T(4,128)S(1)} %get-tuple-element.26, f32[4]{0:T(128)S(1)} %add_rsqrt_fusion, f32[16]{0:T(128)S(1)} %eq.96, f32[4]{0:T(128)S(1)} %iota_convert_fusion), kind=kOutput, calls=%fused_computation.49 | convolution fusion | flops 98880 | bytes 10336 | tf_op jit(solution)/shard_map/dot_general | solution.py:97
  71.9 3.3 %all-to-all-start.3 = ((f32[8,2,128]{2,1,0:T(2,128)}), f32[8,2,128]{2,1,0:T(2,128)S(1)}, u32[]{:S(2)}, u32[]{:S(2)}) async-start(f32[8,2,128]{2,1,0:T(2,128)} %bitcast.11), calls=%async_computation.3 | async-start | bytes 16384 | tf_op jit(solution)/shard_map/all_to_all | solution.py:98
  75.2 0.8 copy.74
  76.0 6.8 %all-to-all-done.3 = f32[8,2,128]{2,1,0:T(2,128)S(1)} async-done(((f32[8,2,128]{2,1,0:T(2,128)}), f32[8,2,128]{2,1,0:T(2,128)S(1)}, u32[]{:S(2)}, u32[]{:S(2)}) %all-to-all-start.3) | async-done | bytes 8224 | tf_op jit(solution)/shard_map/all_to_all | solution.py:98
  82.9 0.1 copy.71
  83.0 0.4 fusion.27
  83.3 0.3 fusion.6
  83.6 0.2 fusion.8
  83.8 0.6 fusion.18
  (33 shorter events, 0.5 us)
Async XLA Ops:
  3.2 6.7 %copy-start.1 = (f32[8,256]{1,0:T(8,128)S(1)}, f32[8,256]{1,0:T(8,128)}, u32[]{:S(2)}) copy-start(f32[8,256]{1,0:T(8,128)} %param.13) | copy-start | bytes 24580
  3.2 6.8 %copy-start.5 = (s32[8,1]{0,1:T(1,128)S(1)}, s32[8,1]{0,1:T(1,128)}, u32[]{:S(2)}) copy-start(s32[8,1]{0,1:T(1,128)} %param.14) | copy-start | bytes 100
  3.2 7.0 %copy-start.6 = (s32[8]{0:T(128)S(1)}, s32[8]{0:T(128)}, u32[]{:S(2)}) copy-start(s32[8]{0:T(128)} %param.15) | copy-start | bytes 100
  3.2 7.7 %copy-start.2 = (f32[8,6,256]{2,0,1:T(8,128)S(1)}, f32[8,6,256]{2,0,1:T(8,128)}, u32[]{:S(2)}) copy-start(f32[8,6,256]{2,0,1:T(8,128)} %param.12) | copy-start | bytes 147460
  3.2 7.8 %slice-start = ((f32[8,6,256]{2,0,1:T(8,128)}), f32[8,3,256]{2,0,1:T(8,128)S(1)}, s32[]{:S(2)}) async-start(f32[8,6,256]{2,0,1:T(8,128)} %param.12), calls=%async_computation.4 | async-start | bytes 49152 | tf_op jit(solution)/shard_map/slice | solution.py:12
  3.2 7.9 %copy-start = (bf16[8,32,256]{2,1,0:T(8,128)(2,1)S(1)}, bf16[8,32,256]{2,1,0:T(8,128)(2,1)}, u32[]{:S(2)}) copy-start(bf16[8,32,256]{2,1,0:T(8,128)(2,1)} %param.8) | copy-start | bytes 393220
  3.2 41.2 %copy-start.3 = (s32[48]{0:T(128)S(1)}, s32[48]{0:T(128)}, u32[]{:S(2)}) copy-start(s32[48]{0:T(128)} %param.11) | copy-start | bytes 580
  3.2 34.5 %all-to-all-start = ((bf16[16,8,8192]{2,1,0:T(8,128)(2,1)}), bf16[16,8,8192]{2,1,0:T(8,128)(2,1)S(1)}, u32[]{:S(2)}, u32[]{:S(2)}) async-start(bf16[16,8,8192]{2,1,0:T(8,128)(2,1)} %stack.4), calls=%async_computation | async-start | bytes 4194304 | tf_op jit(solution)/shard_map/all_to_all | solution.py:42
  37.7 18.1 %all-to-all-start.1 = ((f32[8,1,2]{2,1,0:T(1,128)}), f32[8,1,2]{2,1,0:T(1,128)S(1)}, u32[]{:S(2)}, u32[]{:S(2)}) async-start(f32[8,1,2]{2,1,0:T(1,128)} %bitcast.4), calls=%async_computation.1 | async-start | bytes 8192 | tf_op jit(solution)/shard_map/all_to_all | solution.py:90
  52.1 0.7 copy-start.4
  55.8 14.9 %all-to-all-start.2 = ((f32[8,2,128]{2,1,0:T(2,128)}), f32[8,2,128]{2,1,0:T(2,128)S(1)}, u32[]{:S(2)}, u32[]{:S(2)}) async-start(f32[8,2,128]{2,1,0:T(2,128)} %copy.70), calls=%async_computation.2 | async-start | bytes 16384 | tf_op jit(solution)/shard_map/all_to_all | solution.py:89
  71.9 11.0 %all-to-all-start.3 = ((f32[8,2,128]{2,1,0:T(2,128)}), f32[8,2,128]{2,1,0:T(2,128)S(1)}, u32[]{:S(2)}, u32[]{:S(2)}) async-start(f32[8,2,128]{2,1,0:T(2,128)} %bitcast.11), calls=%async_computation.3 | async-start | bytes 16384 | tf_op jit(solution)/shard_map/all_to_all | solution.py:98
